TPU v7x, 128 devices: a whole 4x4x4 slice. The times are simulated.
128 devices in a mesh: gx: 8 (over y, core), gy: 16 (over z, x).
Axes of the slice: x: 4, y: 4, z: 4, core: 2. Of those that a mesh axis runs over, the one named last changes fastest.
Arguments:
- displacement: float32 [3, 192, 128, 128], P(None, 'gx', 'gy'), may hold values from -6 to 6
- velocity: float32 [3, 192, 128, 128], P(None, 'gx', 'gy'), may hold values from -6 to 6
- external_force: float32 [3, 192, 128, 128], P(None, 'gx', 'gy'), may hold values from -6 to 6
- node_mass: float32 [192, 128, 128], P('gx', 'gy'), may hold values from 0.5 to 2
- stiffness: float32 [192, 128, 128], P('gx', 'gy'), may hold values from 0.5 to 2
- cloak_list: int32 [8, 16, 48], P('gx'), may hold values from -1 to 191, as said below
- micro_state: float32 [8, 16, 128, 48, 128], P('gx', 'gy'), may hold values from -6 to 6
- localization: float32 [256, 6], replicated, may hold values from -3.6 to 3.6
- modes: float32 [256, 128], replicated, may hold values from -0.5 to 0.5
- point_weight: float32 [256], replicated, may hold values from 0.5 to 2
- point_modulus: float32 [256], replicated, may hold values from 1 to 10
- softening: float32 [256], replicated, may hold values from 0.2 to 2
Outputs:
- displacement_next: float32 [3, 192, 128, 128], P(None, 'gx', 'gy')
- velocity_next: float32 [3, 192, 128, 128], P(None, 'gx', 'gy')
- micro_state_next: float32 [8, 16, 128, 48, 128], P('gx', 'gy')
Inputs may be any that keep to these rules, and one draw needn't show every extreme that they name: cloak_list[p, t, :] holds distinct pencil indices x * 8 + y of tile (p, t) in ascending order followed by -1; in every gx index exactly one tile lists 48 pencils and every other tile lists between 22 and 24 pencils, 22 reached in every gx index; the tiles sharing a gx index list exactly 384 pencils together.
All inputs are finite; a program needn't handle non-finite values.
Results may differ from a plain program's by a relative error of at most 0.0003.
Values sent between devices are 32-bit elements; how exact they have to be, the bound alone decides.
A program may use at most 64 MiB of HBM per device.

v0:
```python
import functools

import jax
import jax.numpy as jnp
from jax import lax
from jax.experimental import pallas as pl
from jax.experimental.pallas import tpu as pltpu
from jax.sharding import PartitionSpec as P

ITERS = 3
STEP = 0.25
F32 = jnp.float32
BF16 = jnp.bfloat16
MESH = pl.DeviceIdType.MESH
VMEM = pl.BlockSpec(memory_space=pltpu.VMEM)
SMEM = pl.BlockSpec(memory_space=pltpu.SMEM)
ANY = pl.BlockSpec(memory_space=pl.ANY)


def split(x):
    high = x.astype(BF16)
    low = (x - high.astype(F32)).astype(BF16)
    return high, low


def dot(a, b):
    return jnp.dot(a, b, preferred_element_type=F32)


def dot3(a, b):
    ah, al = split(a)
    bh, bl = split(b)
    return dot(jnp.concatenate([ah, ah, al], axis=1), jnp.concatenate([bh, bl, bh], axis=0))


def dot6(a, b):
    return jnp.dot(a, b, preferred_element_type=F32, precision=lax.Precision.HIGHEST)


def eye(n):
    rows = lax.broadcasted_iota(jnp.int32, (n, n), 0)
    columns = lax.broadcasted_iota(jnp.int32, (n, n), 1)
    return rows == columns


def total_square(x):
    return jnp.sum(jnp.sum(x * x, axis=0, keepdims=True), axis=1, keepdims=True)


def start_inverse(matrix, rounds):
    n = matrix.shape[0]
    diagonal = eye(n)
    unit = jnp.where(diagonal, 1.0, 0.0).astype(F32)
    inv_row = lax.rsqrt(jnp.sum(jnp.where(diagonal, matrix, 0.0), axis=0, keepdims=True))
    inv_column = lax.rsqrt(jnp.sum(jnp.where(diagonal, matrix, 0.0), axis=1, keepdims=True))
    scaled = matrix * inv_row * inv_column
    square = dot3(scaled, scaled)
    bound = jnp.max(jnp.sum(jnp.abs(square), axis=0, keepdims=True), axis=1, keepdims=True)
    c = 1.9 * lax.rsqrt(bound)
    x = (2.0 * c) * unit - (c * c) * scaled
    rest = unit - (2.0 * c) * scaled + (c * c) * square
    for _ in range(rounds):
        x = x + dot3(x, rest)
        rest = unit - dot3(scaled, x)
    return scaled, inv_column, x, rest


def finish_inverse(scaled, x, error):
    unit = jnp.where(eye(x.shape[0]), 1.0, 0.0).astype(F32)

    def unfinished(carry):
        count, error, _ = carry
        return jnp.logical_and(error > 1e-3, count < 40)

    def improve(carry):
        count, _, x = carry
        x = x + dot3(x, unit - dot3(scaled, x))
        rest = unit - dot3(scaled, x)
        return count + 1, jnp.sum(rest * rest), x

    _, _, x = lax.while_loop(unfinished, improve, (0, error, x))
    for _ in range(2):
        x = x + dot6(x, unit - dot6(scaled, x))
    return x


def neighbours():
    n_gx, n_gy = lax.axis_size("gx"), lax.axis_size("gy")
    gx, gy = lax.axis_index("gx"), lax.axis_index("gy")
    up = (lax.rem(gx + 1, n_gx), lax.rem(gy + 1, n_gy))
    down = (lax.rem(gx + n_gx - 1, n_gx), lax.rem(gy + n_gy - 1, n_gy))
    senders = [(up[0], gy), (gx, up[1]), up]
    targets = [(down[0], gy), (gx, down[1]), down]
    return senders, targets


def meet(others):
    barrier = pltpu.get_barrier_semaphore()
    for device in others:
        pl.semaphore_signal(barrier, inc=1, device_id=device, device_id_type=MESH)
    return barrier


def prepare_kernel(disp, modes_ref, loc_ref, weight_ref, modulus_ref, soft_ref,
                   w_ref, t_ref, scaled_ref, x_ref, column_ref, error_ref, project_ref, hx_ref, hy_ref, hc_ref,
                   loc_pad, rx, ry, rc, send_sem, recv_sem):
    uppers, lowers = neighbours()
    barrier = meet(uppers + lowers)
    loc_pad[...] = jnp.zeros_like(loc_pad)
    loc_pad[0:6, :] = loc_ref[...]
    pl.semaphore_wait(barrier, 6)
    copies = []
    for slot, (source, target, device) in enumerate([
        (disp.at[:, 0], rx, lowers[0]),
        (disp.at[:, :, 0:1], ry, lowers[1]),
        (disp.at[:, 0, 0:1], rc, lowers[2]),
    ]):
        copy = pltpu.make_async_remote_copy(
            src_ref=source, dst_ref=target, send_sem=send_sem.at[slot], recv_sem=recv_sem.at[slot],
            device_id=device, device_id_type=MESH)
        copy.start()
        copies.append(copy)

    points, m = modes_ref.shape
    modes = modes_ref[...]
    modes_t = modes.T
    loc_t = loc_pad[...]
    soft = soft_ref[...]
    inv_root = lax.rsqrt(soft)
    root = soft * inv_root
    weights = weight_ref[...] * modulus_ref[...] * (1.0 / points)
    scaled, inv_column, x, rest = start_inverse(dot6(modes_t * weights, modes), 6)
    scaled_ref[...] = scaled
    x_ref[...] = x
    column_ref[...] = -inv_column
    error_ref[...] = jnp.broadcast_to(total_square(rest), error_ref.shape)
    project_ref[...] = modes_t * (weights * inv_root) * inv_column
    t = jnp.concatenate([loc_t * (weights * inv_root), jnp.zeros((8, points), F32)], axis=0)
    th, tl = split(t)
    t_ref[...] = jnp.concatenate([th, th, tl], axis=1)
    mh, ml = split((modes_t * root).T)
    w_ref[:, 0:m] = mh
    w_ref[:, m : 2 * m] = mh
    w_ref[:, 2 * m : 3 * m] = ml
    lh = (loc_t * root).astype(BF16).astype(F32)
    ll = loc_t * root - lh
    local = jnp.concatenate([lh, lh, ll, jnp.zeros((m - 24, points), F32)], axis=0)
    w_ref[:, 3 * m : 4 * m] = local.T.astype(BF16)

    for copy in copies:
        copy.wait()
    last_x = lax.axis_index("gx") == lax.axis_size("gx") - 1
    last_y = lax.axis_index("gy") == lax.axis_size("gy") - 1
    keep_x = jnp.where(last_x, 0.0, 1.0)
    keep_y = jnp.where(last_y, 0.0, 1.0)
    hx_ref[...] = rx[...] * keep_x
    for row in range(hy_ref.shape[1]):
        hy_ref[:, row : row + 1, :] = ry[:, row] * keep_y
    hc_ref[...] = rc[...] * (keep_x * keep_y)


def prepare(disp, modes, loc, weight, modulus, soft):
    points, m = modes.shape
    rows, cols, layers = disp.shape[1:]
    row = lambda x: x.reshape(1, points)
    return pl.pallas_call(
        prepare_kernel,
        out_shape=(
            jax.ShapeDtypeStruct((points, 4 * m), BF16),
            jax.ShapeDtypeStruct((16, 3 * points), BF16),
            jax.ShapeDtypeStruct((m, m), F32),
            jax.ShapeDtypeStruct((m, m), F32),
            jax.ShapeDtypeStruct((m, 1), F32),
            jax.ShapeDtypeStruct((8, 128), F32),
            jax.ShapeDtypeStruct((m, points), F32),
            jax.ShapeDtypeStruct((3, cols, layers), F32),
            jax.ShapeDtypeStruct((3, rows, layers), F32),
            jax.ShapeDtypeStruct((3, 1, layers), F32),
        ),
        in_specs=[ANY] + [VMEM] * 5,
        out_specs=(VMEM,) * 10,
        scratch_shapes=[
            pltpu.VMEM((8, points), F32),
            pltpu.VMEM((3, cols, layers), F32),
            pltpu.VMEM((3, rows, 1, layers), F32),
            pltpu.VMEM((3, 1, layers), F32),
            pltpu.SemaphoreType.DMA((3,)),
            pltpu.SemaphoreType.DMA((3,)),
        ],
        compiler_params=pltpu.CompilerParams(collective_id=0, has_side_effects=True),
        name="prepare",
    )(disp, modes, loc.T, row(weight), row(modulus), row(soft))


def micro_kernel(list_ref, w_ref, t_ref, scaled_ref, x_ref, column_ref, error_ref, project_ref, hx_ref, hy_ref, hc_ref, disp_ref, stiff_ref, state_hbm,
                 new_hbm, force_ref, ex_ref, ey_ref, ec_ref,
                 g_ref, state, strain, stress, in_sem, out_sem):
    rows, cols, layers = stiff_ref.shape
    blocks = state.shape[0]
    m = state.shape[1] // 8
    points = w_ref.shape[0]
    member = lax.axis_index("gy")

    def fetch(b):
        return pltpu.make_async_copy(
            state_hbm.at[:, pl.ds(b * 8, 8), :], state.at[b].reshape(m, 8, layers), in_sem.at[b])

    def drain(b):
        return pltpu.make_async_copy(
            state.at[b].reshape(m, 8, layers), new_hbm.at[:, pl.ds(b * 8, 8), :], out_sem.at[b])

    for b in range(blocks):
        fetch(b).start()

    inverse = finish_inverse(scaled_ref[...], x_ref[...], error_ref[0, 0])
    gh, gl = split(column_ref[...] * dot6(inverse, project_ref[...]))
    g_ref[...] = jnp.concatenate([gh, gh, gl], axis=1)

    lane = lax.broadcasted_iota(jnp.int32, (cols, layers), 1)
    sub = lax.broadcasted_iota(jnp.int32, (cols, layers), 0)
    last_lane = lane == layers - 1
    first_lane = lane == 0
    last_sub = sub == cols - 1
    first_sub = sub == 0

    def node_terms(values, beyond):
        out = []
        for c in range(3):
            here = values[c]
            there = jnp.where(last_sub, beyond[c], pltpu.roll(here, cols - 1, 0))
            total = here + there
            slope = there - here
            above = jnp.where(last_lane, 0.0, pltpu.roll(total, layers - 1, 1))
            slope_above = jnp.where(last_lane, 0.0, pltpu.roll(slope, layers - 1, 1))
            out.append((total + above, slope + slope_above, above - total))
        return out

    def element_row(x, low, high):
        first = [0.25 * (high[c][0] - low[c][0]) for c in range(3)]
        second = [0.25 * (high[c][1] + low[c][1]) for c in range(3)]
        third = [0.25 * (high[c][2] + low[c][2]) for c in range(3)]
        e = [first[0], second[1], third[2], third[1] + second[2], third[0] + first[2], second[0] + first[1]]
        stiff = stiff_ref[x]
        volume = e[0] + e[1] + e[2]
        s = [stiff * (volume + 2.0 * e[c]) for c in range(3)] + [stiff * e[c] for c in range(3, 6)]
        for c in range(6):
            place = pl.ds(x * cols * 8 + c, cols, stride=8)
            strain[place, :] = e[c]
            stress[place, :] = s[c]
        for c in (6, 7):
            strain[pl.ds(x * cols * 8 + c, cols, stride=8), :] = jnp.zeros((cols, layers), F32)

    terms = node_terms([disp_ref[c, 0] for c in range(3)], [hy_ref[c, 0:1, :] for c in range(3)])
    for x in range(rows):
        if x + 1 < rows:
            later = node_terms([disp_ref[c, x + 1] for c in range(3)], [hy_ref[c, x + 1 : x + 2, :] for c in range(3)])
        else:
            later = node_terms([hx_ref[c] for c in range(3)], [hc_ref[c] for c in range(3)])
        element_row(x, terms, later)
        terms = later
    dummy = rows * cols
    strain[pl.ds(dummy * 8, 8), :] = jnp.zeros((8, layers), F32)

    def place_of(e):
        entry = list_ref[0, member, e]
        return entry >= 0, pl.multiple_of(jnp.where(entry >= 0, entry, dummy) * 8, 8)

    def sub_chunk(b, j):
        pair = [place_of(b * 8 + j + i) for i in range(2)]
        a = jnp.concatenate([state[b, pl.ds(j + i, m, stride=8), :] for i in range(2)], axis=1)
        e = jnp.concatenate([strain[pl.ds(pair[i][1], 8), :] for i in range(2)], axis=1)
        return pair, a, e

    def solve(chunks):
        u, a = [], []
        for _, amp, e in chunks:
            ah, al = split(amp)
            eh = e.astype(BF16).astype(F32)
            tail = jnp.concatenate([eh, e - eh], axis=0).astype(BF16)
            head = jnp.concatenate([eh, jnp.zeros_like(eh)], axis=0).astype(BF16)
            rhs = jnp.concatenate([ah, al, ah, tail, head], axis=0)
            u.append(dot(w_ref[:, 0 : 3 * m + 32], rhs))
            a.append(amp)
        count = len(chunks)
        for _ in range(ITERS):
            deltas = []
            for c in range(count):
                rh, rl = split(u[c] * lax.rsqrt(1.0 + u[c] * u[c]))
                deltas.append(dot(g_ref[...], jnp.concatenate([rh, rl, rh], axis=0)))
            for c in range(count):
                dh, dl = split(deltas[c])
                a[c] = a[c] + deltas[c]
                u[c] = u[c] + dot(w_ref[:, 0 : 3 * m], jnp.concatenate([dh, dl, dh], axis=0))
        out = []
        for c in range(count):
            rh, rl = split(u[c] * lax.rsqrt(1.0 + u[c] * u[c]))
            out.append(dot(t_ref[...], jnp.concatenate([rh, rl, rh], axis=0)))
        return a, out

    total = jnp.int32(0)
    for e in range(blocks * 8):
        total = total + jnp.where(list_ref[0, member, e] >= 0, 1, 0)

    def block_step(b, carry):
        fetch(b).wait()
        for half in range(2):
            base = b * 8 + half * 4

            @pl.when(base < total)
            def _():
                chunks = [sub_chunk(b, half * 4 + 2 * c) for c in range(2)]
                a, out = solve(chunks)
                for c in range(2):
                    for i in range(2):
                        listed, place = chunks[c][0][i]
                        columns = slice(i * layers, (i + 1) * layers)
                        keep = jnp.where(listed, 1.0, 0.0)
                        state[b, pl.ds(half * 4 + 2 * c + i, m, stride=8), :] = a[c][:, columns] * keep
                        stress[pl.ds(place, 8), :] = out[c][0:8, columns]

            @pl.when(base >= total)
            def _():
                for i in range(4):
                    state[b, pl.ds(half * 4 + i, m, stride=8), :] = jnp.zeros((m, layers), F32)

        drain(b).start()
        return carry

    lax.fori_loop(0, blocks, block_step, 0)

    def element_terms(x):
        s = [stress[pl.ds(x * cols * 8 + c, cols, stride=8), :] for c in range(6)]
        below = [jnp.where(first_lane, 0.0, pltpu.roll(s[c], 1, 1)) for c in range(6)]
        zsum = [s[c] + below[c] for c in range(6)]
        zdiff = [s[c] - below[c] for c in range(6)]
        p = [zsum[0], zsum[5], zsum[4]]
        q = [zsum[5], zsum[1], zsum[3]]
        r = [zdiff[4], zdiff[3], zdiff[2]]
        out = []
        for i in range(3):
            plus, minus = r[i] + q[i], r[i] - q[i]
            out.append((plus + p[i], plus - p[i], minus + p[i], minus - p[i]))
        return out

    def node_row(own, above):
        rolled = pltpu.roll(above, 1, 0)
        return -0.25 * (own + jnp.where(first_sub, 0.0, rolled)), -0.25 * rolled[0:1, :]

    zero = jnp.zeros((cols, layers), F32)
    before = [(zero, zero)] * 3
    for x in range(rows):
        terms = element_terms(x)
        for i in range(3):
            inner, edge = node_row(terms[i][0] + before[i][0], terms[i][2] + before[i][1])
            force_ref[i, x] = inner
            ey_ref[i, x : x + 1, :] = edge
        before = [(terms[i][1], terms[i][3]) for i in range(3)]
    for i in range(3):
        inner, edge = node_row(before[i][0], before[i][1])
        ex_ref[i] = inner
        ec_ref[i] = edge
    for b in range(blocks):
        drain(b).wait()


def micro(cloak_list, constants, halos, disp, stiff, state):
    m, slots, layers = state.shape
    rows, cols, _ = stiff.shape
    blocks = slots // 8
    return pl.pallas_call(
        micro_kernel,
        out_shape=(
            jax.ShapeDtypeStruct(state.shape, F32),
            jax.ShapeDtypeStruct((3, rows, cols, layers), F32),
            jax.ShapeDtypeStruct((3, cols, layers), F32),
            jax.ShapeDtypeStruct((3, rows, layers), F32),
            jax.ShapeDtypeStruct((3, 1, layers), F32),
        ),
        in_specs=[SMEM] + [VMEM] * 12 + [ANY],
        out_specs=(ANY, VMEM, VMEM, VMEM, VMEM),
        scratch_shapes=[
            pltpu.VMEM((m, constants[1].shape[1]), BF16),
            pltpu.VMEM((blocks, m * 8, layers), F32),
            pltpu.VMEM(((rows * cols + 1) * 8, layers), F32),
            pltpu.VMEM(((rows * cols + 1) * 8, layers), F32),
            pltpu.SemaphoreType.DMA((blocks,)),
            pltpu.SemaphoreType.DMA((blocks,)),
        ],
        name="micro",
    )(cloak_list, *constants, *halos, disp, stiff, state)


def join_kernel(force_ref, ex_ref, ey_ref, ec_ref, out_ref, rx, ry, rc, send_sem, recv_sem):
    uppers, lowers = neighbours()
    barrier = meet(uppers + lowers)
    pl.semaphore_wait(barrier, 6)
    copies = []
    for slot, (source, target, device) in enumerate([
        (ex_ref, rx, uppers[0]), (ey_ref, ry, uppers[1]), (ec_ref, rc, uppers[2]),
    ]):
        copy = pltpu.make_async_remote_copy(
            src_ref=source, dst_ref=target, send_sem=send_sem.at[slot], recv_sem=recv_sem.at[slot],
            device_id=device, device_id_type=MESH)
        copy.start()
        copies.append(copy)
    out_ref[...] = force_ref[...]
    for copy in copies:
        copy.wait()
    keep_x = jnp.where(lax.axis_index("gx") == 0, 0.0, 1.0)
    keep_y = jnp.where(lax.axis_index("gy") == 0, 0.0, 1.0)
    out_ref[:, 0] = out_ref[:, 0] + rx[...] * keep_x
    for i in range(3):
        out_ref[i, :, 0, :] = out_ref[i, :, 0, :] + ry[i] * keep_y
        out_ref[i, 0, 0:1, :] = out_ref[i, 0, 0:1, :] + rc[i] * (keep_x * keep_y)


def join(force, ex, ey, ec):
    return pl.pallas_call(
        join_kernel,
        out_shape=jax.ShapeDtypeStruct(force.shape, F32),
        in_specs=[VMEM] * 4,
        out_specs=VMEM,
        scratch_shapes=[
            pltpu.VMEM(ex.shape, F32),
            pltpu.VMEM(ey.shape, F32),
            pltpu.VMEM(ec.shape, F32),
            pltpu.SemaphoreType.DMA((3,)),
            pltpu.SemaphoreType.DMA((3,)),
        ],
        compiler_params=pltpu.CompilerParams(collective_id=1, has_side_effects=True),
        name="join",
    )(force, ex, ey, ec)


def on_device(displacement, velocity, external_force, node_mass, stiffness, cloak_list, micro_state,
              localization, modes, point_weight, point_modulus, softening):
    prepared = prepare(displacement, modes, localization, point_weight, point_modulus, softening)
    new_state, force, ex, ey, ec = micro(
        cloak_list, prepared[:7], prepared[7:], displacement, stiffness, micro_state[0, 0])
    internal = join(force, ex, ey, ec)
    velocity_next = velocity + STEP * (external_force - internal) / node_mass[None]
    displacement_next = displacement + STEP * velocity_next
    return displacement_next, velocity_next, new_state[None, None]


def solution(mesh):
    grid = P(None, "gx", "gy", None)
    tile = P("gx", "gy", None)
    state = P("gx", "gy", None, None, None)
    return jax.shard_map(
        on_device,
        mesh=mesh,
        in_specs=(grid, grid, grid, tile, tile, P("gx", None, None), state, P(), P(), P(), P(), P()),
        out_specs=(grid, grid, state),
        check_vma=False,
    )
```

profile of v0, /device:TPU:1, one launch (start us, length us, event | category | flops | bytes accessed | tf_op | source)
XLA Modules:
  0.0 57.9 jit_solution(17452991618681480266)
XLA Ops:
  0.6 0.0 copy-start
  0.6 0.0 copy-start.3
  0.7 0.0 copy-start.2
  0.7 0.0 copy-start.1
  0.7 12.5 %prepare.1 = (bf16[256,512]{1,0:T(8,128)(2,1)}, bf16[16,768]{1,0:T(8,128)(2,1)}, f32[128,128]{1,0:T(8,128)}, f32[128,128]{1,0:T(8,128)}, f32[128,1]{1,0:T(8,128)...) custom-call(f32[3,24,8,128]{3,2,1,0:T(8,128)} %disp_ref.1, ...), custom_call_target="tpu_custom_call" | custom-call | tf_op jit(solution)/shard_map/prepare/pallas_call | solution.py:166
  13.2 19.2 %micro.1 = (f32[128,48,128]{2,1,0:T(8,128)}, f32[3,24,8,128]{3,2,1,0:T(8,128)}, f32[3,8,128]{2,1,0:T(8,128)}, f32[3,24,128]{2,1,0:T(8,128)}, f32[3,1,128]{2,1,0:T(1,128)}) custom-call(s32[1,16,48]{2,1,0:T(8,128)} %list_ref.1, bf16[256,512]{1,0:T(8,128)(2,1)} %get-tuple-element.18.w_ref, bf16[16,768]{1,0:T(8,128)(2,1)} %get-tuple-element.19.t_ref, ...), custom_call_target="tpu_custom_call" | custom-call | tf_op jit(solution)/shard_map/micro/pallas_call | solution.py:370
  32.4 23.6 %join.1 = f32[3,24,8,128]{3,2,1,0:T(8,128)} custom-call(f32[3,24,8,128]{3,2,1,0:T(8,128)} %get-tuple-element.28.force_ref, f32[3,8,128]{2,1,0:T(8,128)} %get-tuple-element.29.ex_ref, f32[3,24,128]{2,1,0:T(8,128)} %get-tuple-element.30.ey_ref, f32[3,1,128]{2,1,0:T(1,128)} %get-tuple-element.31.ec_ref), custom_call_target="tpu_custom_call" | custom-call | tf_op jit(solution)/shard_map/join/pallas_call | solution.py:418
  56.1 0.0 copy-done
  56.1 0.0 copy-done.3
  56.1 0.0 copy-done.2
  56.1 0.0 copy-done.1
  56.1 1.8 %multiply_add_fusion = (f32[3,24,8,128]{3,2,1,0:T(8,128)}, f32[3,24,8,128]{3,2,1,0:T(8,128)}) fusion(f32[3,24,8,128]{3,2,1,0:T(8,128)S(1)} %copy-done, f32[3,24,8,128]{3,2,1,0:T(8,128)S(1)} %copy-done.1, f32[24,8,128]{2,1,0:T(8,128)S(1)} %copy-done.3, f32[3,24,8,128]{3,2,1,0:T(8,128)S(1)} %copy-done.2, f32[3,24,8,128]{3,2,1,0:T(8,128)} %join.1), kind=kLoop, calls=%fused_computation | loop fusion | flops 442368 | bytes 1867776 | tf_op jit(solution)/shard_map/add | solution.py:442
Async XLA Ops:
  0.6 55.4 %copy-start = (f32[3,24,8,128]{3,2,1,0:T(8,128)S(1)}, f32[3,24,8,128]{3,2,1,0:T(8,128)}, u32[]{:S(2)}) copy-start(f32[3,24,8,128]{3,2,1,0:T(8,128)} %disp_ref.1) | copy-start | bytes 884740
  0.6 55.4 %copy-start.3 = (f32[24,8,128]{2,1,0:T(8,128)S(1)}, f32[24,8,128]{2,1,0:T(8,128)}, u32[]{:S(2)}) copy-start(f32[24,8,128]{2,1,0:T(8,128)} %param.15) | copy-start | bytes 294916
  0.7 55.4 %copy-start.2 = (f32[3,24,8,128]{3,2,1,0:T(8,128)S(1)}, f32[3,24,8,128]{3,2,1,0:T(8,128)}, u32[]{:S(2)}) copy-start(f32[3,24,8,128]{3,2,1,0:T(8,128)} %param.14) | copy-start | bytes 884740
  0.7 55.4 %copy-start.1 = (f32[3,24,8,128]{3,2,1,0:T(8,128)S(1)}, f32[3,24,8,128]{3,2,1,0:T(8,128)}, u32[]{:S(2)}) copy-start(f32[3,24,8,128]{3,2,1,0:T(8,128)} %param.13) | copy-start | bytes 884740
where the time goes:
time: 58.2 us; the launch traced here: 57.9 us
  Pallas kernels  55.4 us (95%)
  other arithmetic  1.84 us (3%)
  between operations  0.72 us (1%)
    pallas_call x1, Pallas kernels, join(): pl.pallas_call(join_kernel, out_shape=jax.ShapeDtypeStruct(force.shape, F...  23.6 us
    pallas_call x1, Pallas kernels, micro(): pl.pallas_call(micro_kernel, out_shape=(jax.ShapeDtypeStruct(state.shape,...  19.2 us
    pallas_call x1, Pallas kernels, prepare(): pl.pallas_call(prepare_kernel, out_shape=(jax.ShapeDtypeStruct((points, 4...  12.5 us
    add x1, other arithmetic, on_device(): displacement_next = displacement + STEP * velocity_next  1.84 us

commit v1 on v0

--- a/solution.py
+++ b/solution.py
@@ -194,7 +194,7 @@
 
 def micro_kernel(list_ref, w_ref, t_ref, scaled_ref, x_ref, column_ref, error_ref, project_ref, hx_ref, hy_ref, hc_ref, disp_ref, stiff_ref, state_hbm,
                  new_hbm, force_ref, ex_ref, ey_ref, ec_ref,
-                 g_ref, state, strain, stress, in_sem, out_sem):
+                 g_ref, h_ref, state, strain, stress, in_sem, out_sem):
     rows, cols, layers = stiff_ref.shape
     blocks = state.shape[0]
     m = state.shape[1] // 8
@@ -215,6 +215,8 @@
     inverse = finish_inverse(scaled_ref[...], x_ref[...], error_ref[0, 0])
     gh, gl = split(column_ref[...] * dot6(inverse, project_ref[...]))
     g_ref[...] = jnp.concatenate([gh, gh, gl], axis=1)
+    hh, hl = split(dot(w_ref[:, 0 : 3 * m], jnp.concatenate([gh, gl, gh], axis=0)))
+    h_ref[...] = jnp.concatenate([hh, hh, hl], axis=1)
 
     lane = lax.broadcasted_iota(jnp.int32, (cols, layers), 1)
     sub = lax.broadcasted_iota(jnp.int32, (cols, layers), 0)
@@ -272,26 +274,30 @@
         return pair, a, e
 
     def solve(chunks):
-        u, a = [], []
+        u, sums = [], []
         for _, amp, e in chunks:
             ah, al = split(amp)
             eh = e.astype(BF16).astype(F32)
             tail = jnp.concatenate([eh, e - eh], axis=0).astype(BF16)
             head = jnp.concatenate([eh, jnp.zeros_like(eh)], axis=0).astype(BF16)
-            rhs = jnp.concatenate([ah, al, ah, tail, head], axis=0)
-            u.append(dot(w_ref[:, 0 : 3 * m + 32], rhs))
-            a.append(amp)
+            u.append(dot(w_ref[:, 0 : 3 * m + 32], jnp.concatenate([ah, al, ah, tail, head], axis=0)))
         count = len(chunks)
-        for _ in range(ITERS):
-            deltas = []
+        for step in range(ITERS):
             for c in range(count):
-                rh, rl = split(u[c] * lax.rsqrt(1.0 + u[c] * u[c]))
-                deltas.append(dot(g_ref[...], jnp.concatenate([rh, rl, rh], axis=0)))
-            for c in range(count):
-                dh, dl = split(deltas[c])
-                a[c] = a[c] + deltas[c]
-                u[c] = u[c] + dot(w_ref[:, 0 : 3 * m], jnp.concatenate([dh, dl, dh], axis=0))
-        out = []
+                r = u[c] * lax.rsqrt(1.0 + u[c] * u[c])
+                if step < ITERS - 1:
+                    rh, rl = split(r)
+                    u[c] = u[c] + dot(h_ref[...], jnp.concatenate([rh, rl, rh], axis=0))
+                else:
+                    u[c] = u[c] + dot(h_ref[:, 0:points], r.astype(BF16))
+                if step == 0:
+                    sums.append(r)
+                else:
+                    sums[c] = sums[c] + r
+        a, out = [], []
+        for c in range(count):
+            sh, sl = split(sums[c])
+            a.append(chunks[c][1] + dot(g_ref[...], jnp.concatenate([sh, sl, sh], axis=0)))
         for c in range(count):
             rh, rl = split(u[c] * lax.rsqrt(1.0 + u[c] * u[c]))
             out.append(dot(t_ref[...], jnp.concatenate([rh, rl, rh], axis=0)))
@@ -303,25 +309,23 @@
 
     def block_step(b, carry):
         fetch(b).wait()
-        for half in range(2):
-            base = b * 8 + half * 4
-
-            @pl.when(base < total)
-            def _():
-                chunks = [sub_chunk(b, half * 4 + 2 * c) for c in range(2)]
-                a, out = solve(chunks)
-                for c in range(2):
-                    for i in range(2):
-                        listed, place = chunks[c][0][i]
-                        columns = slice(i * layers, (i + 1) * layers)
-                        keep = jnp.where(listed, 1.0, 0.0)
-                        state[b, pl.ds(half * 4 + 2 * c + i, m, stride=8), :] = a[c][:, columns] * keep
-                        stress[pl.ds(place, 8), :] = out[c][0:8, columns]
-
-            @pl.when(base >= total)
-            def _():
-                for i in range(4):
-                    state[b, pl.ds(half * 4 + i, m, stride=8), :] = jnp.zeros((m, layers), F32)
+        base = b * 8
+
+        @pl.when(base < total)
+        def _():
+            chunks = [sub_chunk(b, 2 * c) for c in range(4)]
+            a, out = solve(chunks)
+            for c in range(4):
+                for i in range(2):
+                    listed, place = chunks[c][0][i]
+                    columns = slice(i * layers, (i + 1) * layers)
+                    keep = jnp.where(listed, 1.0, 0.0)
+                    state[b, pl.ds(2 * c + i, m, stride=8), :] = a[c][:, columns] * keep
+                    stress[pl.ds(place, 8), :] = out[c][0:8, columns]
+
+        @pl.when(base >= total)
+        def _():
+            state[b] = jnp.zeros((m * 8, layers), F32)
 
         drain(b).start()
         return carry
@@ -380,6 +384,7 @@
         out_specs=(ANY, VMEM, VMEM, VMEM, VMEM),
         scratch_shapes=[
             pltpu.VMEM((m, constants[1].shape[1]), BF16),
+            pltpu.VMEM((constants[0].shape[0], constants[1].shape[1]), BF16),
             pltpu.VMEM((blocks, m * 8, layers), F32),
             pltpu.VMEM(((rows * cols + 1) * 8, layers), F32),
             pltpu.VMEM(((rows * cols + 1) * 8, layers), F32),

time: 58.2 us -> 43.4 us (0.75)
  Pallas kernels: 55.4 us -> 40.5 us
    pallas_call x1, Pallas kernels: 23.6 us -> 15.4 us  [join(): pl.pallas_call(join_kernel, out_shape=jax.ShapeDtypeStruct(force.shape, F...]
    pallas_call x1, Pallas kernels: 19.2 us -> 12.6 us  [micro(): pl.pallas_call(micro_kernel, out_shape=(jax.ShapeDtypeStruct(state.shape,...]
where the time goes in v1:
time: 43.4 us; the launch traced here: 43.1 us
  Pallas kernels  40.5 us (93%)
  other arithmetic  1.84 us (4%)
  between operations  0.72 us (2%)
    pallas_call x1, Pallas kernels, join(): pl.pallas_call(join_kernel, out_shape=jax.ShapeDtypeStruct(force.shape, F...  15.4 us
    pallas_call x1, Pallas kernels, micro(): pl.pallas_call(micro_kernel, out_shape=(jax.ShapeDtypeStruct(state.shape,...  12.6 us
    pallas_call x1, Pallas kernels, prepare(): pl.pallas_call(prepare_kernel, out_shape=(jax.ShapeDtypeStruct((points, 4...  12.5 us
    add x1, other arithmetic, on_device(): displacement_next = displacement + STEP * velocity_next  1.84 us

profile of v1, /device:TPU:1, one launch (start us, length us, event | category | flops | bytes accessed | tf_op | source)
XLA Modules:
  0.0 43.1 jit_solution(16222303481993711279)
XLA Ops:
  0.6 0.0 copy-start
  0.6 0.0 copy-start.3
  0.7 0.0 copy-start.2
  0.7 0.0 copy-start.1
  0.7 12.5 %prepare.1 = (bf16[256,512]{1,0:T(8,128)(2,1)}, bf16[16,768]{1,0:T(8,128)(2,1)}, f32[128,128]{1,0:T(8,128)}, f32[128,128]{1,0:T(8,128)}, f32[128,1]{1,0:T(8,128)...) custom-call(f32[3,24,8,128]{3,2,1,0:T(8,128)} %disp_ref.1, ...), custom_call_target="tpu_custom_call" | custom-call | tf_op jit(solution)/shard_map/prepare/pallas_call | solution.py:166
  13.2 12.6 %micro.1 = (f32[128,48,128]{2,1,0:T(8,128)}, f32[3,24,8,128]{3,2,1,0:T(8,128)}, f32[3,8,128]{2,1,0:T(8,128)}, f32[3,24,128]{2,1,0:T(8,128)}, f32[3,1,128]{2,1,0:T(1,128)}) custom-call(s32[1,16,48]{2,1,0:T(8,128)} %list_ref.1, bf16[256,512]{1,0:T(8,128)(2,1)} %get-tuple-element.18.w_ref, bf16[16,768]{1,0:T(8,128)(2,1)} %get-tuple-element.19.t_ref, ...), custom_call_target="tpu_custom_call" | custom-call | tf_op jit(solution)/shard_map/micro/pallas_call | solution.py:374
  25.8 15.4 %join.1 = f32[3,24,8,128]{3,2,1,0:T(8,128)} custom-call(f32[3,24,8,128]{3,2,1,0:T(8,128)} %get-tuple-element.28.force_ref, f32[3,8,128]{2,1,0:T(8,128)} %get-tuple-element.29.ex_ref, f32[3,24,128]{2,1,0:T(8,128)} %get-tuple-element.30.ey_ref, f32[3,1,128]{2,1,0:T(1,128)} %get-tuple-element.31.ec_ref), custom_call_target="tpu_custom_call" | custom-call | tf_op jit(solution)/shard_map/join/pallas_call | solution.py:423
  41.2 0.0 copy-done
  41.2 0.0 copy-done.3
  41.3 0.0 copy-done.2
  41.3 0.0 copy-done.1
  41.3 1.8 %multiply_add_fusion = (f32[3,24,8,128]{3,2,1,0:T(8,128)}, f32[3,24,8,128]{3,2,1,0:T(8,128)}) fusion(f32[3,24,8,128]{3,2,1,0:T(8,128)S(1)} %copy-done, f32[3,24,8,128]{3,2,1,0:T(8,128)S(1)} %copy-done.1, f32[24,8,128]{2,1,0:T(8,128)S(1)} %copy-done.3, f32[3,24,8,128]{3,2,1,0:T(8,128)S(1)} %copy-done.2, f32[3,24,8,128]{3,2,1,0:T(8,128)} %join.1), kind=kLoop, calls=%fused_computation | loop fusion | flops 442368 | bytes 1867776 | tf_op jit(solution)/shard_map/add | solution.py:447
Async XLA Ops:
  0.6 40.6 %copy-start = (f32[3,24,8,128]{3,2,1,0:T(8,128)S(1)}, f32[3,24,8,128]{3,2,1,0:T(8,128)}, u32[]{:S(2)}) copy-start(f32[3,24,8,128]{3,2,1,0:T(8,128)} %disp_ref.1) | copy-start | bytes 884740
  0.6 40.6 %copy-start.3 = (f32[24,8,128]{2,1,0:T(8,128)S(1)}, f32[24,8,128]{2,1,0:T(8,128)}, u32[]{:S(2)}) copy-start(f32[24,8,128]{2,1,0:T(8,128)} %param.15) | copy-start | bytes 294916
  0.7 40.6 %copy-start.2 = (f32[3,24,8,128]{3,2,1,0:T(8,128)S(1)}, f32[3,24,8,128]{3,2,1,0:T(8,128)}, u32[]{:S(2)}) copy-start(f32[3,24,8,128]{3,2,1,0:T(8,128)} %param.14) | copy-start | bytes 884740
  0.7 40.6 %copy-start.1 = (f32[3,24,8,128]{3,2,1,0:T(8,128)S(1)}, f32[3,24,8,128]{3,2,1,0:T(8,128)}, u32[]{:S(2)}) copy-start(f32[3,24,8,128]{3,2,1,0:T(8,128)} %param.13) | copy-start | bytes 884740
